TPU v7x, 256 devices: a whole 4x4x8 slice. The times are simulated.
256 devices in a mesh: ctx: 64 (over z, x, core), head: 4 (over y).
Axes of the slice: x: 4, y: 4, z: 8, core: 2. Of those that a mesh axis runs over, the one named last changes fastest.
Arguments:
- queries: bfloat16 [32768, 2048], P('ctx', 'head'), may hold values from -6 to 6
- keys: bfloat16 [32768, 2048], P('ctx', 'head'), may hold values from -6 to 6
- values: bfloat16 [32768, 2048], P('ctx', 'head'), may hold values from -6 to 6
- out_grad: bfloat16 [32768, 2048], P('ctx', 'head'), may hold values from -6 to 6
- inputs: bfloat16 [32768, 4096], P('ctx', 'head'), may hold values from -16 to 16
- value_weight: bfloat16 [4096, 2048], P('ctx', 'head'), may hold values from -0.25 to 0.25
Outputs:
- query_grad: bfloat16 [32768, 2048], P('ctx', 'head')
- key_grad: bfloat16 [32768, 2048], P('ctx', 'head')
- input_grad: bfloat16 [32768, 4096], P('ctx', 'head')
- weight_grad: float32 [4096, 2048], P('ctx', 'head')
All inputs are finite; a program needn't handle non-finite values.
Results may differ from a plain program's by a relative error of at most 0.0049.
Values may be sent and summed in bfloat16 or wider, within the bound.
A program may use at most 128 MiB of HBM per device.

v0:
```python
import math

import jax
import jax.numpy as jnp
from jax import lax
from jax.sharding import PartitionSpec as P

DH = 128


def entering(shard, axis, combine, identity, reverse):
    size, here = (lax.axis_size(axis), lax.axis_index(axis))
    everything = lax.all_gather(shard, axis)
    start = jnp.broadcast_to(jnp.asarray(identity, shard.dtype), shard.shape)

    def lap(k, before):
        at = size - 1 - k if reverse else k
        reached = at > here if reverse else at < here
        new = combine(before, everything[at])
        return jnp.where(reached, new, before)

    return lax.fori_loop(0, size, lap, start)


def add_states(earlier, later_part):
    return earlier + later_part


def local(queries, keys, values, out_grad, inputs, value_weight):
    length = queries.shape[0]
    heads = queries.shape[1] // DH
    factor = 1.0 / math.sqrt(DH * length * lax.axis_size("ctx"))
    highest = lax.Precision.HIGHEST
    query_heads = queries.reshape(length, heads, DH)
    key_heads = keys.reshape(length, heads, DH)
    value_heads = values.reshape(length, heads, DH)
    grad_heads = out_grad.reshape(length, heads, DH)
    local_kv = jnp.einsum(
        "thd,the->hde", key_heads, value_heads, preferred_element_type=jnp.float32
    )
    local_qg = jnp.einsum(
        "thd,the->hde", query_heads, grad_heads, preferred_element_type=jnp.float32
    )
    zeros = jnp.zeros((heads, DH, DH), jnp.float32)
    prior = entering(local_kv, "ctx", add_states, zeros, False)
    later = entering(local_qg, "ctx", add_states, zeros, True)
    rows = lax.broadcasted_iota(jnp.int32, (length, length), 0)
    cols = lax.broadcasted_iota(jnp.int32, (length, length), 1)
    causal = (rows >= cols)[None]
    grad_scores = jnp.where(
        causal,
        jnp.einsum("the,she->hts", grad_heads, value_heads, preferred_element_type=jnp.float32),
        0.0,
    ).astype(jnp.bfloat16)
    key_scores = jnp.where(
        causal,
        jnp.einsum("thd,shd->hts", query_heads, key_heads, preferred_element_type=jnp.float32),
        0.0,
    ).astype(jnp.bfloat16)
    query_out = factor * (
        jnp.einsum("the,hde->thd", grad_heads.astype(jnp.float32), prior, precision=highest)
        + jnp.einsum("hts,shd->thd", grad_scores, key_heads, preferred_element_type=jnp.float32)
    )
    key_out = factor * (
        jnp.einsum("hts,thd->shd", grad_scores, query_heads, preferred_element_type=jnp.float32)
        + jnp.einsum("she,hde->shd", value_heads.astype(jnp.float32), later, precision=highest)
    )
    value_out = factor * (
        jnp.einsum("hts,the->she", key_scores, grad_heads, preferred_element_type=jnp.float32)
        + jnp.einsum("shd,hde->she", key_heads.astype(jnp.float32), later, precision=highest)
    )
    query_grad = query_out.astype(jnp.bfloat16).reshape(length, heads * DH)
    key_grad = key_out.astype(jnp.bfloat16).reshape(length, heads * DH)
    value_grad = value_out.astype(jnp.bfloat16).reshape(length, heads * DH)
    features = lax.all_gather(inputs, "head", axis=1, tiled=True)
    summed = lax.psum_scatter(
        lax.dot_general(
            features, value_grad, (((0,), (0,)), ((), ())), preferred_element_type=jnp.float32
        ),
        "ctx",
        scatter_dimension=0,
        tiled=True,
    )
    weight_grad = summed * (1.0 / math.sqrt(length * lax.axis_size("ctx")))
    partial_grad = lax.dot_general(
        value_grad,
        lax.all_gather(value_weight, "ctx", axis=0, tiled=True),
        (((1,), (1,)), ((), ())),
        preferred_element_type=jnp.float32,
    )
    input_grad = lax.psum_scatter(partial_grad, "head", scatter_dimension=1, tiled=True).astype(
        jnp.bfloat16
    )
    return (query_grad, key_grad, input_grad, weight_grad)


def solution(mesh):
    return jax.shard_map(
        local,
        mesh=mesh,
        in_specs=(
            P("ctx", "head"),
            P("ctx", "head"),
            P("ctx", "head"),
            P("ctx", "head"),
            P("ctx", "head"),
            P("ctx", "head"),
        ),
        out_specs=(P("ctx", "head"), P("ctx", "head"), P("ctx", "head"), P("ctx", "head")),
        check_vma=False,
    )
```

profile of v0, /device:TPU:17, one launch (start us, length us, event | category | flops | bytes accessed | tf_op | source)
XLA Modules:
  0.0 589.5 jit_solution(12524585922660291966)
XLA Ops:
  7.2 1.3 copy.46
  8.6 2.3 fusion.11
  12.4 2.1 fusion.18
  14.7 99.0 %all-gather.13.cloned.1.call-done = f32[256,128,128]{2,1,0:T(8,128)} async-done(((f32[4,128,128]{2,1,0:T(8,128)}), f32[256,128,128]{2,1,0:T(8,128)}) %all-gather.13.cloned.1.call-update) | async-done | bytes 16777232 | tf_op jit(solution)/shard_map/all_gather | solution.py:13
  113.8 68.6 %while.31 = (s32[]{:T(128)}, f32[4,128,128]{2,1,0:T(8,128)S(1)}, s32[]{:T(128)}, f32[64,4,128,128]{3,2,1,0:T(8,128)}, s32[]{:T(128)}, /*index=5*/s32[]{:T(128)}, s32[]{:T(128)}, s32[]{:T(128)}) while((s32[]{:T(128)}, f32[4,128,128]{2,1,0:T(8,128)S(1)}, s32[]{:T(128)}, f32[64,4,128,128]{3,2,1,0:T(8,128)}, s32[]{:T(128)}, ...), condition=%wide.region_3.4_spmd.clone, body=%wide.region_2.3_spmd.clone.sunk | while | flops 196616 | bytes 786587 | solution.py:22
  123.4 1.1 add_select_fusion.5
  124.5 1.1 add_select_fusion.5
  125.6 1.1 add_select_fusion.5
  126.7 1.1 add_select_fusion.5
  182.4 1.6 convolution_bitcast_fusion.3
  184.0 2.3 fusion.10
  186.4 7.8 %convolution_bitcast_fusion = f32[4096,512]{0,1:T(8,128)} fusion(bf16[512,512]{0,1:T(8,128)(2,1)S(1)} %bitcast.124, bf16[512,4096]{1,0:T(8,128)(2,1)} %all-gather.9.cloned.1.call-done), kind=kOutput, calls=%fused_computation.2 | convolution fusion | flops 2147483648 | bytes 13107200 | tf_op jit(solution)/shard_map/dot_general | solution.py:77
  194.2 9.0 %copy.44 = f32[4096,512]{1,0:T(8,128)} copy(f32[4096,512]{0,1:T(8,128)} %convolution_bitcast_fusion) | data formatting | bytes 16777216
  203.2 42.3 %all-gather.7.cloned.1.call-done = bf16[4096,512]{1,0:T(8,128)(2,1)} async-done(((bf16[64,512]{1,0:T(8,128)(2,1)}), bf16[4096,512]{1,0:T(8,128)(2,1)}) %all-gather.7.cloned.1.call-update) | async-done | bytes 4194320 | tf_op jit(solution)/shard_map/all_gather | solution.py:87
  245.5 7.8 %fusion.38 = f32[512,4096]{1,0:T(8,128)} fusion(bf16[512,512]{0,1:T(8,128)(2,1)S(1)} %bitcast.125, bf16[4096,512]{1,0:T(8,128)(2,1)} %all-gather.7.cloned.1.call-done), kind=kOutput, calls=%fused_computation.46 | convolution fusion | flops 2147483648 | bytes 13107200 | tf_op jit(solution)/shard_map/dot_general | solution.py:85
  254.3 1.9 select_convert_fusion.1
  256.2 1.6 convolution_bitcast_fusion.1
  257.8 2.8 convolution_bitcast_fusion.2
  262.3 82.3 %all-gather.11.cloned.1.call-done = f32[256,128,128]{2,1,0:T(8,128)} async-done(((f32[4,128,128]{2,1,0:T(8,128)}), f32[256,128,128]{2,1,0:T(8,128)}) %all-gather.11.cloned.1.call-update) | async-done | bytes 16777232 | tf_op jit(solution)/shard_map/all_gather | solution.py:13
  344.6 68.4 %while.30 = (s32[]{:T(128)}, f32[4,128,128]{2,1,0:T(8,128)S(1)}, s32[]{:T(128)}, f32[64,4,128,128]{3,2,1,0:T(8,128)}, s32[]{:T(128)}, /*index=5*/s32[]{:T(128)}) while((s32[]{:T(128)}, f32[4,128,128]{2,1,0:T(8,128)S(1)}, s32[]{:T(128)}, f32[64,4,128,128]{3,2,1,0:T(8,128)}, s32[]{:T(128)}, /*index=5*/s32[]{:T(128)}) %tuple.91), condition=%wide.region_1.2_spmd.clone, body=%wide.region_0.1_spmd.clone.sunk | while | flops 196612 | bytes 786525 | solution.py:22
  357.3 1.1 add_select_fusion.4
  367.0 1.1 add_select_fusion.4
  369.1 1.1 add_select_fusion.4
  371.3 1.1 add_select_fusion.4
  372.4 1.0 add_select_fusion.4
  373.4 1.1 add_select_fusion.4
  374.5 1.0 add_select_fusion.4
  375.6 1.1 add_select_fusion.4
  376.7 1.0 add_select_fusion.4
  414.6 78.7 %reduce-scatter.7.cloned.1.call-done = f32[64,512]{1,0:T(8,128)} async-done(((f32[4096,512]{1,0:T(8,128)}), f32[64,512]{1,0:T(8,128)}) %reduce-scatter.7.cloned.1.call-update) | async-done | bytes 131088
  495.1 84.8 %reduce-scatter.5.cloned.1.call-done = f32[512,1024]{1,0:T(8,128)} async-done(((f32[512,4096]{1,0:T(8,128)}), f32[512,1024]{1,0:T(8,128)}) %reduce-scatter.5.cloned.1.call-update) | async-done | bytes 2097168 | tf_op jit(solution)/shard_map/reduce_scatter | solution.py:91
  579.9 2.7 convert_element_type.26
  (154 shorter events, 127.7 us)
Async XLA Ops:
  7.2 5.3 copy-start
  7.2 106.6 %all-gather.13.cloned.1.call-start = ((), (), s32[]{:S(2)}) async-start(), calls=%async_computation.6 | async-start | bytes 17039360 | tf_op jit(solution)/shard_map/all_gather | solution.py:13
  8.5 175.5 %copy-start.1 = (bf16[512,512]{0,1:T(8,128)(2,1)}, bf16[512,512]{0,1:T(8,128)(2,1)S(1)}, u32[]{:S(2)}) copy-start(bf16[512,512]{0,1:T(8,128)(2,1)S(1)} %copy.46) | copy-start | bytes 1572868
  8.5 173.9 %copy-start.4 = (bf16[512,512]{1,0:T(8,128)(2,1)S(1)}, bf16[512,512]{1,0:T(8,128)(2,1)}, u32[]{:S(2)}) copy-start(bf16[512,512]{1,0:T(8,128)(2,1)} %param.11) | copy-start | bytes 1572868
  10.9 175.5 %all-gather.9.cloned.1.call-start = ((), (), s32[]{:S(2)}) async-start(), calls=%async_computation.4 | async-start | bytes 5242880 | tf_op jit(solution)/shard_map/all_gather | solution.py:75
  11.6 172.4 %copy-start.5 = (bf16[512,512]{1,0:T(8,128)(2,1)S(1)}, bf16[512,512]{1,0:T(8,128)(2,1)}, u32[]{:S(2)}) copy-start(bf16[512,512]{1,0:T(8,128)(2,1)} %param.10) | copy-start | bytes 1572868
  11.6 233.9 %all-gather.7.cloned.1.call-start = ((), (), s32[]{:S(2)}) async-start(), calls=%async_computation.2 | async-start | bytes 4259840 | tf_op jit(solution)/shard_map/all_gather | solution.py:87
  12.4 332.2 %all-gather.11.cloned.1.call-start = ((), (), s32[]{:S(2)}) async-start(), calls=%async_computation.5 | async-start | bytes 17039360 | tf_op jit(solution)/shard_map/all_gather | solution.py:13
  14.6 478.7 %reduce-scatter.7.cloned.1.call-start = ((), (), s32[]{:S(2)}) async-start(), calls=%async_computation.7 | async-start | bytes 8519680
  14.7 171.6 %copy-start.6 = (pred[512,512]{1,0:T(8,128)(4,1)}, pred[512,512]{1,0:T(8,128)(4,1)S(1)}, u32[]{:S(2)}) copy-start(pred[512,512]{1,0:T(8,128)(4,1)S(1)} %iota_compare_fusion) | copy-start | bytes 786436
  203.2 376.7 %reduce-scatter.5.cloned.1.call-start = ((), (), s32[]{:S(2)}) async-start(), calls=%async_computation.3 | async-start | bytes 10485760 | tf_op jit(solution)/shard_map/reduce_scatter | solution.py:91
  253.4 0.9 copy-start.7
  260.6 152.4 %copy-start.2 = (bf16[512,512]{0,1:T(8,128)(2,1)S(1)}, bf16[512,512]{0,1:T(8,128)(2,1)}, u32[]{:S(2)}) copy-start(bf16[512,512]{0,1:T(8,128)(2,1)} %copy-done.1) | copy-start | bytes 1572868
  260.6 152.4 %copy-start.3 = (f32[512,4,128]{0,2,1:T(8,128)S(1)}, f32[512,4,128]{0,2,1:T(8,128)}, u32[]{:S(2)}) copy-start(f32[512,4,128]{0,2,1:T(8,128)} %convolution_bitcast_fusion.2) | copy-start | bytes 3145732
Sparse Core Ops, SparseCore 0:
  11.3 102.3 all-gather.12
  115.6 46.2 all-gather.8
  164.7 80.8 all-gather.6
  248.2 96.3 all-gather.10
  348.6 144.6 reduce-scatter.6
  495.8 84.0 reduce-scatter.4
where the time goes:
time: 597 us; the launch traced here: 589 us
  waiting for transfers between devices  389 us (65%)
  other arithmetic  137 us (23%)
  matrix products  31.4 us (5%)
  local copies, waits for them, and re-layouts  15.1 us (3%)
  between operations  14.3 us (2%)
    all_gather x2, waiting for transfers between devices, entering(): everything = lax.all_gather(shard, axis)  181 us
    select_n x128, other arithmetic, lap(): return jnp.where(reached, new, before)  134 us
    reduce_scatter x1, waiting for transfers between devices, local(): lax.psum_scatter(partial_grad, 'head', scatter_dimension=1, tiled=True)  84.8 us
    unnamed x7, waiting for transfers between devices  80.1 us
    all_gather x1, waiting for transfers between devices, local(): lax.all_gather(value_weight, 'ctx', axis=0, tiled=True)  42.3 us
    unnamed x21, local copies, waits for them, and re-layouts  13.8 us
  transfers between devices with their start and end apart: 6, of which 5 were waited for; matrix products, arithmetic and copies ran while one was open for 30% of the time, Pallas kernels for 0%

commit v1 on v0

v1 whole, which is shorter than its diff:
```python
import functools
import math

import jax
import jax.numpy as jnp
from jax import lax
from jax.experimental import pallas as pl
from jax.experimental.pallas import tpu as pltpu
from jax.sharding import PartitionSpec as P

DH = 128
NX, NZ, NC, NY = 4, 8, 2, 4
F32, BF16 = jnp.float32, jnp.bfloat16
MESH = pl.DeviceIdType.MESH
NT = (((1,), (1,)), ((), ()))
NN = (((1,), (0,)), ((), ()))


def mm(a, b, dims=NN):
    return lax.dot_general(a, b, dims, preferred_element_type=F32)


def kernel(
    factor, wscale,
    q_hbm, k_hbm, v_hbm, g_hbm, in_hbm, w_hbm,
    q_out, k_out, i_out, w_out,
    qh, kh, vh, gh, inb, int_, wz, wbuf,
    sq, sk, r1q, r1k, wsq, wsk, t2q, t2k, z2q, z2k, zaq, zak, o3q, o3k, later, prior,
    qloc, kloc, vloc, vgall, vsib, part, acc,
    sxa, sxb, sxc, rxa, rxb, rxc, yrecv, ysend, zrecv,
    lsem, ssem, p1sem, p2sem, p3sem, w1sem, w2sem, w3sem, w4sem, isem, ysem, svsem, xsem, ymsem, zsem,
):
    c, h = lax.axis_index("ctx"), lax.axis_index("head")
    z, m = c // 8, c % 8
    x, kk = m // 2, m % 2

    def cidx(zz, xx, cc):
        return zz * 8 + xx * 2 + cc

    sib = cidx(z, x, 1 - kk)
    xr, xl = (x + 1) % NX, (x + 3) % NX
    yr, yl, yo = (h + 1) % NY, (h + 3) % NY, (h + 2) % NY

    pending = []
    count = [0]

    def send(src, dst, rsem, ctx, head, cond=None):
        desc = pltpu.make_async_remote_copy(
            src_ref=src, dst_ref=dst, send_sem=ssem.at[count[0]], recv_sem=rsem,
            device_id=(ctx, head), device_id_type=MESH)
        count[0] += 1
        if cond is None:
            desc.start()
        else:
            pl.when(cond)(desc.start)
        pending.append((cond, desc))

    def arrived(dst, sem, cond=None):
        desc = pltpu.make_async_copy(dst, dst, sem)
        if cond is None:
            desc.wait()
        else:
            pl.when(cond)(desc.wait)

    loads = {}
    n = 0
    for j in range(4):
        for name, src, dst in (("q", q_hbm, qh), ("g", g_hbm, gh)):
            loads[name, j] = pltpu.make_async_copy(src.at[:, pl.ds(DH * j, DH)], dst.at[j], lsem.at[n])
            n += 1
    for j in range(4):
        for name, src, dst in (("k", k_hbm, kh), ("v", v_hbm, vh)):
            loads[name, j] = pltpu.make_async_copy(src.at[:, pl.ds(DH * j, DH)], dst.at[j], lsem.at[n])
            n += 1
    loads["w"] = pltpu.make_async_copy(w_hbm, wz.at[z], lsem.at[n])
    loads["i"] = pltpu.make_async_copy(in_hbm, inb.at[0], lsem.at[n + 1])
    for desc in loads.values():
        desc.start()

    barrier = pltpu.get_barrier_semaphore()
    partners = 0

    def greet(ctx, head):
        pl.semaphore_signal(barrier, inc=1, device_id=(ctx, head), device_id_type=MESH)

    for off in range(1, 8):
        mm_ = (m + off) % 8
        greet(z * 8 + mm_, h)
        partners += 1
    for off in range(1, 8):
        zz = (z + off) % NZ
        for cc in range(NC):
            greet(cidx(zz, x, cc), h)
            partners += 1
    for off in range(1, 4):
        greet(c, (h + off) % NY)
        partners += 1

    for j in range(4):
        loads["q", j].wait()
        loads["g", j].wait()
        sq[j] = mm(qh[j].T, gh[j]).astype(BF16)
    pl.semaphore_wait(barrier, partners)

    def scan1(s, r1, row):
        for off in range(1, 8):
            to = (m + off) % 8
            send(s.at[to // 2, pl.ds(pl.multiple_of(64 * (to % 2), 64), 64)], r1.at[m],
                 p1sem.at[row, off], z * 8 + to, h)
        r1[m] = s[x, pl.ds(pl.multiple_of(64 * kk, 64), 64), :]

    def scan2(r1, ws, t2, z2, row, reverse):
        for off in range(1, 8):
            arrived(r1.at[(m + 8 - off) % 8], p1sem.at[row, off])
        total = jnp.zeros((64, DH), F32)
        order = range(7, -1, -1) if reverse else range(8)
        for i in order:
            ws[i] = total
            total = total + r1[i].astype(F32)
        t2[...] = total
        for d in range(1, NZ):
            zz = z - d if reverse else z + d
            cond = zz >= 0 if reverse else zz < NZ
            send(t2, z2.at[d], p2sem.at[row, d], cidx(jnp.clip(zz, 0, NZ - 1), x, kk), h, cond)

    def scan3(ws, z2, za, o3, full, row, reverse):
        za[...] = jnp.zeros((64, DH), F32)
        for d in range(1, NZ):
            cond = z + d < NZ if reverse else z - d >= 0

            @pl.when(cond)
            def _():
                arrived(z2.at[d], p2sem.at[row, d])
                za[...] += z2[d]
        for i in range(8):
            o3[i] = (ws[i] + za[...]).astype(BF16)
        for off in range(1, 8):
            to = (m + off) % 8
            send(o3.at[to], full.at[x, pl.ds(pl.multiple_of(64 * kk, 64), 64)],
                 p3sem.at[row, off], z * 8 + to, h)
        full[x, pl.ds(pl.multiple_of(64 * kk, 64), 64), :] = o3[m]

    def scan_done(full, row):
        for off in range(1, 8):
            at = (m + 8 - off) % 8
            arrived(full.at[at // 2, pl.ds(pl.multiple_of(64 * (at % 2), 64), 64)], p3sem.at[row, off])

    scan1(sq, r1q, 0)

    loads["w"].wait()
    for off in range(1, NZ):
        send(wz.at[z], wz.at[z], w1sem, cidx((z + off) % NZ, x, kk), h)
    loads["i"].wait()
    send(inb.at[0], inb.at[1], isem, sib, h)

    for j in range(4):
        loads["k", j].wait()
        loads["v", j].wait()
        sk[j] = mm(kh[j].T, vh[j]).astype(BF16)
    scan1(sk, r1k, 1)

    def masked_t(a, b, width):
        s = mm(a, b, NT)
        rows = lax.broadcasted_iota(jnp.int32, (256, width), 0)
        cols = lax.broadcasted_iota(jnp.int32, (256, width), 1)
        return jnp.where(rows <= cols, s, 0.0).astype(BF16)

    def transposed_part(a, b, c_, out):
        def step(j, carry):
            for i in range(2):
                lo = 256 * i
                s = masked_t(a[j, lo:lo + 256, :], b[j, lo:512, :], 512 - lo)
                out[j, lo:lo + 256, :] = mm(s, c_[j, lo:512, :])
            return carry
        lax.fori_loop(0, 4, step, 0)

    def straight_part(a, b, c_, out):
        def step(j, carry):
            for i in range(2):
                lo, hi = 256 * i, 256 * i + 256
                s = mm(a[j, lo:hi, :], b[j, 0:hi, :], NT)
                rows = lax.broadcasted_iota(jnp.int32, (256, hi), 0) + lo
                cols = lax.broadcasted_iota(jnp.int32, (256, hi), 1)
                s = jnp.where(rows >= cols, s, 0.0).astype(BF16)
                out[j, lo:hi, :] = mm(s, c_[j, 0:hi, :])
            return carry
        lax.fori_loop(0, 4, step, 0)

    scan2(r1q, wsq, t2q, z2q, 0, True)
    transposed_part(kh, qh, gh, vloc)
    scan2(r1k, wsk, t2k, z2k, 1, False)

    def transpose_inputs(slot):
        def step(j, carry):
            at = pl.multiple_of(128 * j, 128)
            int_[slot, pl.ds(at, 128), :] = inb[slot, :, pl.ds(at, 128)].T
            return carry
        lax.fori_loop(0, 8, step, 0)

    transpose_inputs(0)
    scan3(wsq, z2q, zaq, o3q, later, 0, True)

    arrived(wz.at[pl.ds(0, 7)], w1sem)
    for off in range(1, NY):
        to = (h + off) % NY
        send(wz.at[pl.ds(2 * to, 2)], wbuf.at[h, :, x, kk], w2sem.at[off], c, to)
    wbuf[h, 0, x, kk] = wz[2 * h]
    wbuf[h, 1, x, kk] = wz[2 * h + 1]

    scan3(wsk, z2k, zak, o3k, prior, 1, False)
    arrived(inb.at[1], isem)

    scan_done(later, 0)
    for cc in range(2):
        for j in (2 * cc, 2 * cc + 1):
            val = factor * (vloc[j] + mm(kh[j], later[j]))
            vgall[h, cc, :, pl.ds(128 * (j % 2), 128)] = val.astype(BF16)
        send(vgall.at[h, cc], vgall.at[h, cc], ysem.at[0, cc], c, yr)
        send(vgall.at[h, cc], vgall.at[h, cc], ysem.at[1, cc], c, yl)
    send(vgall.at[h, 1 - kk], vsib.at[0], svsem.at[0], sib, h)

    for off in range(1, NY):
        arrived(wbuf.at[(h + NY - off) % NY, :, x, kk], w2sem.at[off])
    for b in range(2):
        send(wbuf.at[:, b, x, kk], wbuf.at[:, b, x, kk], w3sem.at[0, b], cidx(z, xr, kk), h)
        send(wbuf.at[:, b, x, kk], wbuf.at[:, b, x, kk], w3sem.at[1, b], cidx(z, xl, kk), h)
    send(wbuf.at[:, :, x, kk], wbuf.at[:, :, x, kk], w4sem.at[0], sib, h)

    transpose_inputs(1)

    origins = (h, yl, yr, yo)
    movers = (h, yl, yr, yo)
    senders = (h, yr, yl, yo)

    def partial(e):
        def step(i, carry):
            rows = pl.ds(pl.multiple_of(256 * i, 256), 256)
            p = mm(int_[0, rows, :], vgall[origins[e], kk]) + mm(int_[1, rows, :], vsib[e])
            b, x0 = i // 2, 2 * (i % 2)
            part[e, x0, b] = p[:128]
            part[e, x0 + 1, b] = p[128:]
            return carry
        lax.fori_loop(0, 4, step, 0)

    def ways(e):
        return (xr, xl) if e % 2 == 0 else (xl, xr)

    def xsend1(e):
        fw, bw = ways(e)
        sxa[e] = part[e, (x + 2) % NX].astype(BF16)
        send(sxa.at[e], rxa.at[e], xsem.at[0, e], cidx(z, fw, kk), h)
        sxb[e] = part[e, bw].astype(BF16)
        send(sxb.at[e], rxb.at[e], xsem.at[1, e], cidx(z, bw, kk), h)

    def xsend2(e):
        fw, bw = ways(e)
        arrived(rxa.at[e], xsem.at[0, e])
        sxc[e] = (part[e, fw] + rxa[e].astype(F32)).astype(BF16)
        send(sxc.at[e], rxc.at[e], xsem.at[2, e], cidx(z, fw, kk), h)

    def zsend(s):
        for b in range(2):
            for kr in range(2):
                to = cidx(2 * senders[s] + b, x, kr)
                send(yrecv.at[s, b, pl.ds(64 * kr, 64)], zrecv.at[z * 2 + kk], zsem, to, h, to != c)

                @pl.when(to == c)
                def _():
                    zrecv[z * 2 + kk] = yrecv[s, b, 64 * kr:64 * kr + 64, :]

    def xdone(e):
        arrived(rxb.at[e], xsem.at[1, e])
        arrived(rxc.at[e], xsem.at[2, e])
        total = part[e, x] + rxb[e].astype(F32) + rxc[e].astype(F32)
        if e == 0:
            yrecv[0] = total.astype(BF16)
            zsend(0)
        else:
            ysend[e] = total.astype(BF16)
            send(ysend.at[e], yrecv.at[e], ymsem.at[e], c, movers[e])

    def ydone(s):
        arrived(yrecv.at[s], ymsem.at[s])
        zsend(s)

    def input_part(e, first):
        o = origins[e]

        def step(i, carry):
            b, x0 = i // 2, 2 * (i % 2)
            w = wbuf[o, b, pl.ds(x0, 2)].reshape(256, 512)
            p = mm(vgall[o, 0], w[:, :256], NT) + mm(vgall[o, 1], w[:, 256:], NT)
            acc[i] = p if first else acc[i] + p
            return carry
        lax.fori_loop(0, 4, step, 0)

    arrived(vsib.at[0], svsem.at[0])
    partial(0)
    xsend1(0)
    transposed_part(vh, gh, qh, kloc)
    xsend2(0)

    def key_step(j, carry):
        at = pl.ds(pl.multiple_of(128 * j, 128), 128)
        k_out[:, at] = (factor * (kloc[j] + mm(vh[j], later[j], NT))).astype(BF16)
        return carry
    lax.fori_loop(0, 4, key_step, 0)

    for b in range(2):
        arrived(wbuf.at[:, b, xl, kk], w3sem.at[0, b])
        if b == 0:
            send(wbuf.at[:, 0, xl, kk], wbuf.at[:, 0, xl, kk], w3sem.at[2, 0], cidx(z, xr, kk), h)
    for b in (1, 0):
        arrived(wbuf.at[:, b, xr, kk], w3sem.at[1, b])
        if b == 1:
            send(wbuf.at[:, 1, xr, kk], wbuf.at[:, 1, xr, kk], w3sem.at[2, 1], cidx(z, xl, kk), h)
    send(wbuf.at[:, :, xl, kk], wbuf.at[:, :, xl, kk], w4sem.at[1], sib, h)
    send(wbuf.at[:, :, xr, kk], wbuf.at[:, :, xr, kk], w4sem.at[2], sib, h)
    xdone(0)

    straight_part(gh, vh, kh, qloc)
    scan_done(prior, 1)

    def query_step(j, carry):
        at = pl.ds(pl.multiple_of(128 * j, 128), 128)
        q_out[:, at] = (factor * (qloc[j] + mm(gh[j], prior[j], NT))).astype(BF16)
        return carry
    lax.fori_loop(0, 4, query_step, 0)

    arrived(vgall.at[yl, 0], ysem.at[0, 0])
    send(vgall.at[yl, 0], vgall.at[yl, 0], ysem.at[2, 0], c, yr)
    arrived(vgall.at[yr, 0], ysem.at[1, 0])
    arrived(vgall.at[yr, 1], ysem.at[1, 1])
    send(vgall.at[yr, 1], vgall.at[yr, 1], ysem.at[2, 1], c, yl)
    arrived(vgall.at[yl, 1], ysem.at[0, 1])
    send(vgall.at[yl, 1 - kk], vsib.at[1], svsem.at[1], sib, h)
    send(vgall.at[yr, 1 - kk], vsib.at[2], svsem.at[2], sib, h)
    arrived(vsib.at[1], svsem.at[1])
    partial(1)
    xsend1(1)
    arrived(vsib.at[2], svsem.at[2])
    partial(2)
    xsend1(2)
    xsend2(1)
    xsend2(2)
    for b in range(2):
        arrived(wbuf.at[:, b, (x + 2) % NX, kk], w3sem.at[2, b])
    send(wbuf.at[:, :, (x + 2) % NX, kk], wbuf.at[:, :, (x + 2) % NX, kk], w4sem.at[3], sib, h)
    xdone(1)
    xdone(2)
    for i, at in enumerate((x, xl, xr, (x + 2) % NX)):
        arrived(wbuf.at[:, :, at, 1 - kk], w4sem.at[i])
    input_part(0, True)
    ydone(1)
    ydone(2)

    arrived(vgall.at[yo, 0], ysem.at[2, 0])
    arrived(vgall.at[yo, 1], ysem.at[2, 1])
    send(vgall.at[yo, 1 - kk], vsib.at[3], svsem.at[3], sib, h)
    arrived(vsib.at[3], svsem.at[3])
    partial(3)
    xsend1(3)
    input_part(1, False)
    xsend2(3)
    input_part(2, False)
    xdone(3)
    input_part(3, False)
    ydone(3)
    for i in range(4):
        i_out[:, 256 * i:256 * i + 256] = acc[i].astype(BF16)

    arrived(zrecv.at[pl.ds(0, 15)], zsem)
    for cc in range(2):
        total = zrecv[cc].astype(F32)
        for zz in range(1, NZ):
            total = total + zrecv[2 * zz + cc].astype(F32)
        w_out[:, 256 * cc:256 * cc + 256] = total * wscale

    for cond, desc in pending:
        if cond is None:
            desc.wait_send()
        else:
            pl.when(cond)(desc.wait_send)


def local(queries, keys, values, out_grad, inputs, value_weight):
    length = queries.shape[0]
    tokens = length * lax.axis_size("ctx")
    factor = 1.0 / math.sqrt(DH * tokens)
    wscale = 1.0 / math.sqrt(tokens)
    vm = pltpu.VMEM
    dma = pltpu.SemaphoreType.DMA
    scratch = [
        vm((4, 512, 128), BF16), vm((4, 512, 128), BF16), vm((4, 512, 128), BF16), vm((4, 512, 128), BF16),
        vm((2, 512, 1024), BF16), vm((2, 1024, 512), BF16),
        vm((8, 64, 512), BF16), vm((4, 2, 4, 2, 64, 512), BF16),
        vm((4, 128, 128), BF16), vm((4, 128, 128), BF16),
        vm((8, 64, 128), BF16), vm((8, 64, 128), BF16),
        vm((8, 64, 128), F32), vm((8, 64, 128), F32),
        vm((64, 128), F32), vm((64, 128), F32),
        vm((8, 64, 128), F32), vm((8, 64, 128), F32),
        vm((64, 128), F32), vm((64, 128), F32),
        vm((8, 64, 128), BF16), vm((8, 64, 128), BF16),
        vm((4, 128, 128), BF16), vm((4, 128, 128), BF16),
        vm((4, 512, 128), F32), vm((4, 512, 128), F32), vm((4, 512, 128), F32),
        vm((4, 2, 512, 256), BF16), vm((4, 512, 256), BF16),
        vm((4, 4, 2, 128, 256), F32), vm((4, 512, 256), F32),
        vm((4, 2, 128, 256), BF16), vm((4, 2, 128, 256), BF16), vm((4, 2, 128, 256), BF16),
        vm((4, 2, 128, 256), BF16), vm((4, 2, 128, 256), BF16), vm((4, 2, 128, 256), BF16),
        vm((4, 2, 128, 256), BF16), vm((4, 2, 128, 256), BF16),
        vm((16, 64, 256), BF16),
        dma((18,)), dma((128,)), dma((2, 8)), dma((2, 8)), dma((2, 8)),
        dma(()), dma((4,)), dma((3, 2)), dma((4,)), dma(()), dma((3, 2)), dma((4,)), dma((3, 4)), dma((4,)), dma(()),
    ]
    out_shape = (
        jax.ShapeDtypeStruct((512, 512), BF16),
        jax.ShapeDtypeStruct((512, 512), BF16),
        jax.ShapeDtypeStruct((512, 1024), BF16),
        jax.ShapeDtypeStruct((64, 512), F32),
    )
    return pl.pallas_call(
        functools.partial(kernel, factor, wscale),
        out_shape=out_shape,
        in_specs=[pl.BlockSpec(memory_space=pl.ANY)] * 6,
        out_specs=[pl.BlockSpec(memory_space=pltpu.VMEM)] * 4,
        scratch_shapes=scratch,
        compiler_params=pltpu.CompilerParams(
            collective_id=0, has_side_effects=True, vmem_limit_bytes=56 * 1024 * 1024),
        name="attention_backward",
    )(queries, keys, values, out_grad, inputs, value_weight)


def solution(mesh):
    spec = P("ctx", "head")
    return jax.shard_map(
        local, mesh=mesh, in_specs=(spec,) * 6, out_specs=(spec,) * 4, check_vma=False)
```

time: 597 us -> 112 us (0.19); the launches traced: 589 us -> 111 us
  waiting for transfers between devices: 389 us -> 0 us
  other arithmetic: 137 us -> 0 us
  Pallas kernels: 0 us -> 105 us
  matrix products: 31.4 us -> 0 us
  between operations: 14.3 us -> 0.65 us
  local copies, waits for them, and re-layouts: 15.1 us -> 5.5 us
    all_gather x4 -> x0, waiting for transfers between devices: 224 us -> none  [the longest x2 181 us: entering(): everything = lax.all_gather(shard, axis)]
    select_n x128 -> x0, other arithmetic: 134 us -> none  [lap(): return jnp.where(reached, new, before)]
    pallas_call x0 -> x1, Pallas kernels: none -> 105 us  [local(): pl.pallas_call(functools.partial(kernel, factor, wscale), out_shape=out_s...]
    reduce_scatter x1 -> x0, waiting for transfers between devices: 84.8 us -> none  [local(): lax.psum_scatter(partial_grad, 'head', scatter_dimension=1, tiled=True)]
    unnamed x7 -> x0, waiting for transfers between devices: 80.1 us -> none
    dot_general x11 -> x0, matrix products: 31.4 us -> none  [the longest x1 7.83 us: local(): lax.dot_general(value_grad, lax.all_gather(value_weight, 'ctx', axis=0, t...]
    unnamed x21 -> x8, local copies, waits for them, and re-layouts: 13.8 us -> 5.5 us
  transfers between devices with their start and end apart: 6 -> 0, of which waited for: 5 -> 0; matrix products, arithmetic and copies ran while one was open for 30% -> 0% of each run, Pallas kernels for 0% -> 0%
where the time goes in v1:
time: 112 us; the launch traced here: 111 us
  Pallas kernels  105 us (94%)
  local copies, waits for them, and re-layouts  5.5 us (5%)
    pallas_call x1, Pallas kernels, local(): pl.pallas_call(functools.partial(kernel, factor, wscale), out_shape=out_s...  105 us
    unnamed x8, local copies, waits for them, and re-layouts  5.5 us

profile of v1, /device:TPU:17, one launch (start us, length us, event | category | flops | bytes accessed | tf_op | source)
XLA Modules:
  0.0 111.5 jit_solution(14558095421713671594)
XLA Ops:
  0.6 105.3 %attention_backward.1 = (bf16[512,512]{1,0:T(8,128)(2,1)}, bf16[512,512]{1,0:T(8,128)(2,1)}, bf16[512,1024]{1,0:T(8,128)(2,1)}, f32[64,512]{1,0:T(8,128)}) custom-call(bf16[512,512]{1,0:T(8,128)(2,1)} %q_hbm.1, bf16[512,512]{1,0:T(8,128)(2,1)} %k_hbm.1, bf16[512,512]{1,0:T(8,128)(2,1)} %v_hbm.1, bf16[512,512]{1,0:T(8,128)(2,1)} %g_hbm.1, ...), custom_call_target="tpu_custom_call" | custom-call | tf_op jit(solution)/shard_map/attention_backward/pallas_call | solution.py:421
  106.0 0.0 copy-start
  106.0 2.0 %copy.14 = bf16[512,512]{1,0:T(8,128)(2,1)} copy(bf16[512,512]{1,0:T(8,128)(2,1)} %get-tuple-element.8) | data formatting | bytes 1048576
  107.9 1.9 %copy.15 = bf16[512,512]{1,0:T(8,128)(2,1)} copy(bf16[512,512]{1,0:T(8,128)(2,1)} %get-tuple-element.9) | data formatting | bytes 1048576
  109.8 0.0 copy-done
  109.8 0.0 copy-start.1
  109.8 1.0 copy.16
  110.8 0.1 copy-done.1
  110.8 0.7 copy.17
Async XLA Ops:
  106.0 3.8 %copy-start = (bf16[512,1024]{1,0:T(8,128)(2,1)S(1)}, bf16[512,1024]{1,0:T(8,128)(2,1)}, u32[]{:S(2)}) copy-start(bf16[512,1024]{1,0:T(8,128)(2,1)} %get-tuple-element.10) | copy-start | bytes 3145732
  109.8 1.0 copy-start.1

commit v2 on v1

v2 whole, which is shorter than its diff:
```python
import functools
import math

import jax
import jax.numpy as jnp
from jax import lax
from jax.experimental import pallas as pl
from jax.experimental.pallas import tpu as pltpu
from jax.sharding import PartitionSpec as P

DH = 128
NX, NZ, NC, NY = 4, 8, 2, 4
F32, BF16 = jnp.float32, jnp.bfloat16
MESH = pl.DeviceIdType.MESH
NT = (((1,), (1,)), ((), ()))
NN = (((1,), (0,)), ((), ()))


def mm(a, b, dims=NN):
    return lax.dot_general(a, b, dims, preferred_element_type=F32)


def kernel(
    factor, wscale,
    q_hbm, k_hbm, v_hbm, g_hbm, in_hbm, w_hbm,
    q_out, k_out, i_out, w_out,
    qh, kh, vh, gh, inb, int_, wz, wbuf,
    sq, sk, r1q, r1k, wsq, wsk, t2q, t2k, z2q, z2k, zaq, zak, o3q, o3k, later, prior,
    qloc, kloc, vloc, vgall, vsib, part, acc,
    sxa, sxb, sxc, rxa, rxb, rxc, zs, zr, zfs, zfr, xfs, xfr, fs, fr, qs, ks, ist,
    lsem, ssem, p1sem, p2sem, p3sem, w1sem, w2sem, w3sem, w4sem, isem, ysem, svsem, xsem, zsem, fsem, osem,
):
    c, h = lax.axis_index("ctx"), lax.axis_index("head")
    z, m = c // 8, c % 8
    x, kk = m // 2, m % 2

    def cidx(zz, xx, cc):
        return zz * 8 + xx * 2 + cc

    sib = cidx(z, x, 1 - kk)
    xr, xl = (x + 1) % NX, (x + 3) % NX
    yr, yl, yo = (h + 1) % NY, (h + 3) % NY, (h + 2) % NY

    pending = []
    count = [0]

    def group(n=1):
        count[0] += n
        return ssem.at[count[0] - n] if n == 1 else [ssem.at[count[0] - n + i] for i in range(n)]

    def send(src, dst, rsem, ctx, head, sem, cond=None):
        desc = pltpu.make_async_remote_copy(
            src_ref=src, dst_ref=dst, send_sem=sem, recv_sem=rsem,
            device_id=(ctx, head), device_id_type=MESH)
        if cond is None:
            desc.start()
        else:
            pl.when(cond)(desc.start)
        return desc

    def sent(ref, sem):
        pending.append((None, pltpu.make_async_copy(ref, ref, sem)))

    def arrived(dst, sem, cond=None):
        desc = pltpu.make_async_copy(dst, dst, sem)
        if cond is None:
            desc.wait()
        else:
            pl.when(cond)(desc.wait)

    for n, (src, dst) in enumerate(((q_hbm, qh), (g_hbm, gh), (k_hbm, kh), (v_hbm, vh))):
        for j in range(4):
            pltpu.make_async_copy(src.at[:, pl.ds(DH * j, DH)], dst.at[j], lsem.at[n]).start()
    load_w = pltpu.make_async_copy(w_hbm, wz.at[z], lsem.at[4])
    load_w.start()
    load_i = pltpu.make_async_copy(in_hbm, inb.at[0], lsem.at[5])
    load_i.start()

    barrier = pltpu.get_barrier_semaphore()
    partners = 0

    def greet(ctx, head):
        pl.semaphore_signal(barrier, inc=1, device_id=(ctx, head), device_id_type=MESH)

    for off in range(1, 8):
        mm_ = (m + off) % 8
        greet(z * 8 + mm_, h)
        partners += 1
    for off in range(1, 8):
        zz = (z + off) % NZ
        greet(cidx(zz, x, kk), h)
        partners += 1
    for off in range(1, 4):
        greet(c, (h + off) % NY)
        partners += 1

    arrived(qh, lsem.at[0])
    arrived(gh, lsem.at[1])
    for j in range(4):
        sq[j] = mm(qh[j].T, gh[j])
    arrived(kh, lsem.at[2])
    arrived(vh, lsem.at[3])
    for j in range(4):
        sk[j] = mm(kh[j].T, vh[j])
    pl.semaphore_wait(barrier, partners)

    def scan1(s, r1, row):
        sem = group()
        for off in range(1, 8):
            to = (m + off) % 8
            send(s.at[to // 2, pl.ds(pl.multiple_of(64 * (to % 2), 64), 64)], r1.at[m],
                 p1sem.at[row], z * 8 + to, h, sem)
        sent(r1.at[pl.ds(0, 7)], sem)
        r1[m] = s[x, pl.ds(pl.multiple_of(64 * kk, 64), 64), :]

    def scan2(r1, ws, t2, z2, row, reverse):
        arrived(r1.at[pl.ds(0, 7)], p1sem.at[row])
        total = jnp.zeros((64, DH), F32)
        order = range(7, -1, -1) if reverse else range(8)
        for i in order:
            ws[i] = total
            total = total + r1[i]
        t2[...] = total.astype(BF16)
        for d in range(1, NZ):
            zz = z - d if reverse else z + d
            cond = zz >= 0 if reverse else zz < NZ
            desc = send(t2, z2.at[d], p2sem.at[row, d], cidx(jnp.clip(zz, 0, NZ - 1), x, kk), h, group(), cond)
            pending.append((cond, desc))

    def scan3(ws, z2, za, o3, full, row, reverse):
        za[...] = jnp.zeros((64, DH), F32)
        for d in range(1, NZ):
            cond = z + d < NZ if reverse else z - d >= 0

            @pl.when(cond)
            def _():
                arrived(z2.at[d], p2sem.at[row, d])
                za[...] += z2[d].astype(F32)
        for i in range(8):
            o3[i] = (ws[i] + za[...]).astype(BF16)
        sem = group()
        for off in range(1, 8):
            to = (m + off) % 8
            send(o3.at[to], full.at[x, pl.ds(pl.multiple_of(64 * kk, 64), 64)],
                 p3sem.at[row], z * 8 + to, h, sem)
        sent(o3.at[pl.ds(0, 7)], sem)
        full[x, pl.ds(pl.multiple_of(64 * kk, 64), 64), :] = o3[m]

    def scan_done(o3, row):
        arrived(o3.at[pl.ds(0, 7)], p3sem.at[row])

    scan1(sq, r1q, 0)

    wnsem, wzsem = group(), group()

    def wnext(zs):
        to = zs // 2
        send(wz.at[zs], wbuf.at[h, zs % 2, x, kk], w2sem, c, to, wnsem, to != h)

        @pl.when(to == h)
        def _():
            wbuf[h, zs % 2, x, kk] = wz[zs]

    def wz_to(at, sem, dz):
        send(wz.at[at], wz.at[at], sem, cidx((z + dz + NZ) % NZ, x, kk), h, wzsem)

    def wring1():
        load_w.wait()
        for d in (1, 2):
            wz_to(z, w1sem.at[0, d], d)
            wz_to(z, w1sem.at[1, d], -d)
        wnext(z)

    def wring2():
        right, left = (z + 6) % NZ, (z + 2) % NZ
        arrived(wz.at[right], w1sem.at[0, 2])
        arrived(wz.at[left], w1sem.at[1, 2])
        wz_to(right, w1sem.at[0, 3], 1)
        wz_to(left, w1sem.at[1, 3], -1)
        wz_to(right, w1sem.at[0, 4], 2)
        wnext(right)
        wnext(left)
        for side, at in ((0, (z + 7) % NZ), (1, (z + 1) % NZ)):
            arrived(wz.at[at], w1sem.at[side, 1])
            wnext(at)

    def wring3():
        for side, d, at in ((0, 3, (z + 5) % NZ), (1, 3, (z + 3) % NZ), (0, 4, (z + 4) % NZ)):
            arrived(wz.at[at], w1sem.at[side, d])
            wnext(at)

    wring1()
    scan1(sk, r1k, 1)
    load_i.wait()
    insem = group()
    send(inb.at[0], inb.at[1], isem, sib, h, insem)
    sent(inb.at[0], insem)

    def masked_t(a, b, width):
        s = mm(a, b, NT)
        rows = lax.broadcasted_iota(jnp.int32, (256, width), 0)
        cols = lax.broadcasted_iota(jnp.int32, (256, width), 1)
        return jnp.where(rows <= cols, s, 0.0).astype(BF16)

    def transposed_part(a, b, c_, out):
        def step(j, carry):
            for i in range(2):
                lo = 256 * i
                s = masked_t(a[j, lo:lo + 256, :], b[j, lo:512, :], 512 - lo)
                out[j, lo:lo + 256, :] = mm(s, c_[j, lo:512, :])
            return carry
        lax.fori_loop(0, 4, step, 0)

    def straight_part(a, b, c_, out):
        def step(j, carry):
            for i in range(2):
                lo, hi = 256 * i, 256 * i + 256
                s = mm(a[j, lo:hi, :], b[j, 0:hi, :], NT)
                rows = lax.broadcasted_iota(jnp.int32, (256, hi), 0) + lo
                cols = lax.broadcasted_iota(jnp.int32, (256, hi), 1)
                s = jnp.where(rows >= cols, s, 0.0).astype(BF16)
                out[j, lo:hi, :] = mm(s, c_[j, 0:hi, :])
            return carry
        lax.fori_loop(0, 4, step, 0)

    def transpose_inputs(slot):
        def step(j, carry):
            at = pl.multiple_of(128 * j, 128)
            int_[slot, pl.ds(at, 128), :] = inb[slot, :, pl.ds(at, 128)].T
            return carry
        lax.fori_loop(0, 8, step, 0)

    sent(wz.at[pl.ds(0, 6)], wnsem)
    sent(wz.at[pl.ds(0, 7)], wzsem)
    scan2(r1q, wsq, t2q, z2q, 0, True)
    wring2()
    transposed_part(kh, qh, gh, vloc)
    scan2(r1k, wsk, t2k, z2k, 1, False)
    transpose_inputs(0)
    arrived(inb.at[1], isem)
    transpose_inputs(1)
    scan3(wsq, z2q, zaq, o3q, later, 0, True)
    wring3()
    scan3(wsk, z2k, zak, o3k, prior, 1, False)

    scan_done(o3q, 0)
    for j in range(4):
        val = factor * (vloc[j] + mm(kh[j], later[j]))
        vgall[h, j] = val.astype(BF16)
    ygsem, yrsem, fwsem = group(), group(), group()
    for j in range(4):
        send(vgall.at[h, j], vgall.at[h, j], ysem.at[0, j], c, yr, ygsem)
        jj = (j + 2) % 4
        send(vgall.at[h, jj], vgall.at[h, jj], ysem.at[1, jj], c, yl, ygsem)
    send(vgall.at[h, pl.ds(2 * (1 - kk), 2)], vsib.at[0], svsem.at[0], sib, h, fwsem)
    sent(vgall.at[pl.ds(0, 2)], ygsem)
    sent(vgall.at[0], yrsem)
    sent(vgall.at[pl.ds(0, 2)], fwsem)

    def pick(first, second):
        return jnp.where(kk == 0, first, second)

    origins = (h, pick(yl, yr), pick(yr, yl), yo, yo)
    sib_origins = (h, origins[2], origins[1], yo, yo)
    heads = ((0, 1), (0, 1), (0, 1), (0,), (1,))
    cols = tuple(128 * len(js) for js in heads)

    def forward(e):
        js = heads[e]
        send(vgall.at[sib_origins[e], pl.ds(2 * (1 - kk) + js[0], len(js))], vsib.at[e, pl.ds(0, len(js))],
             svsem.at[e], sib, h, fwsem)

    def pair(ref, at, j, n):
        if n == 1:
            return ref[at, j]
        return jnp.concatenate([ref[at, j], ref[at, j + 1]], axis=1)

    def partial(e):
        w = cols[e]

        def own(i, carry):
            rows = pl.ds(pl.multiple_of(256 * i, 256), 256)
            p = mm(int_[0, rows, :], pair(vgall, origins[e], 2 * kk + heads[e][0], len(heads[e])))
            b, x0 = i // 2, 2 * (i % 2)
            part[e, x0, b, :, :w] = p[:128]
            part[e, x0 + 1, b, :, :w] = p[128:]
            return carry

        def other(i, carry):
            rows = pl.ds(pl.multiple_of(256 * i, 256), 256)
            p = mm(int_[1, rows, :], pair(vsib, e, 0, len(heads[e])))
            b, x0 = i // 2, 2 * (i % 2)
            part[e, x0, b, :, :w] += p[:128]
            part[e, x0 + 1, b, :, :w] += p[128:]
            return carry

        lax.fori_loop(0, 4, own, 0)
        arrived(vsib.at[e, pl.ds(0, len(heads[e]))], svsem.at[e])
        lax.fori_loop(0, 4, other, 0)

    def ways(e):
        return (xr, xl) if e == 2 else (xl, xr)

    xgsem, zgsem, fgsem, zfsem, xfsem = group(), group(), group(), group(2), group(2)

    def cut(ref, e):
        return ref.at[e, :, :, pl.ds(0, cols[e])]

    def xsend1(e):
        fw, bw = ways(e)
        w = cols[e]
        sxa[e, :, :, :w] = part[e, (x + 2) % NX, :, :, :w].astype(BF16)
        send(cut(sxa, e), cut(rxa, e), xsem.at[0, e], cidx(z, fw, kk), h, xgsem)
        sxb[e, :, :, :w] = part[e, bw, :, :, :w].astype(BF16)
        send(cut(sxb, e), cut(rxb, e), xsem.at[1, e], cidx(z, bw, kk), h, xgsem)

    def xsend2(e):
        fw, bw = ways(e)
        w = cols[e]
        arrived(cut(rxa, e), xsem.at[0, e])
        sxc[e, :, :, :w] = (part[e, fw, :, :, :w] + rxa[e, :, :, :w].astype(F32)).astype(BF16)
        send(cut(sxc, e), cut(rxc, e), xsem.at[2, e], cidx(z, fw, kk), h, xgsem)

    def xdone(e):
        w = cols[e]
        arrived(cut(rxb, e), xsem.at[1, e])
        arrived(cut(rxc, e), xsem.at[2, e])
        for p in range(NZ):
            b, r0 = p % 2, 64 * (p // 2 % 2) + 32 * (p // 4)
            total = (part[e, x, b, r0:r0 + 32, :w] + rxb[e, b, r0:r0 + 32, :w].astype(F32)
                     + rxc[e, b, r0:r0 + 32, :w].astype(F32))
            zs[e, p, :, :w] = total.astype(BF16)
        for dz in range(1, NZ):
            to = (z + dz) % NZ
            send(zs.at[e, to, :, pl.ds(0, w)], zr.at[e, z, :, pl.ds(0, w)], zsem.at[e], cidx(to, x, kk), h, zgsem)
        zr[e, z, :, :w] = zs[e, z, :, :w]

    mine = (h == z // 2) & (kk == z // 2 % 2)
    slot = 2 * kk + z // 4

    def finish(e, total):
        w = cols[e]
        lo = 128 if e == 4 else 0
        fs[e, :, :w] = total * wscale
        to = cidx(2 * h + z % 2, x, z // 2 % 2)
        if e == 0:
            other = jnp.logical_not(mine)
            pending.append((other, send(fs.at[0], fr.at[slot], fsem, to, h, group(), other)))

            @pl.when(mine)
            def _():
                fr[slot] = fs[0]
        else:
            send(fs.at[e, :, pl.ds(0, w)], fr.at[slot, :, pl.ds(lo, w)], fsem, to, origins[e], fgsem)

    def zdone(e):
        w = cols[e]
        arrived(zr.at[e, pl.ds(0, 7), :, pl.ds(0, w)], zsem.at[e])
        total = zr[e, 0, :, :w].astype(F32)
        for zz in range(1, NZ):
            total = total + zr[e, zz, :, :w].astype(F32)
        finish(e, total)

    def zfirst(e):
        for p in range(NZ):
            b, r0 = p % 2, 64 * (p // 2 % 2) + 32 * (p // 4)
            zfs[e, p] = part[e, :, b, r0:r0 + 32, :].astype(BF16)
        for dz in range(1, NZ):
            to = (z + dz) % NZ
            send(zfs.at[e, to], zfr.at[e, z], zsem.at[e], cidx(to, x, kk), h, zfsem[e])
        zfr[e, z] = zfs[e, z]
        sent(zfr.at[e, pl.ds(0, 7)], zfsem[e])

    def xnext(e):
        arrived(zfr.at[e, pl.ds(0, 7)], zsem.at[e])
        for xx in range(NX):
            total = zfr[e, 0, xx].astype(F32)
            for zz in range(1, NZ):
                total = total + zfr[e, zz, xx].astype(F32)
            xfs[e, xx] = total.astype(BF16)
        for dx in range(1, NX):
            to = (x + dx) % NX
            send(xfs.at[e, to], xfr.at[e, x], xsem.at[0, e], cidx(z, to, kk), h, xfsem[e])
        xfr[e, x] = xfs[e, x]
        sent(xfr.at[e, pl.ds(0, 3)], xfsem[e])

    def xlast(e):
        arrived(xfr.at[e, pl.ds(0, 3)], xsem.at[0, e])
        total = xfr[e, 0].astype(F32)
        for xx in range(1, NX):
            total = total + xfr[e, xx].astype(F32)
        finish(e, total)

    def key_step(j, carry):
        at = pl.ds(pl.multiple_of(128 * j, 128), 128)
        ks[:, at] = (factor * (kloc[j] + mm(vh[j], later[j], NT))).astype(BF16)
        return carry

    def query_step(j, carry):
        at = pl.ds(pl.multiple_of(128 * j, 128), 128)
        qs[:, at] = (factor * (qloc[j] + mm(gh[j], prior[j], NT))).astype(BF16)
        return carry

    def put(src, dst, n):
        pltpu.make_async_copy(src, dst, osem.at[n]).start()

    xo = (x + 2) % NX

    def wblock(u, b, at):
        return wbuf.at[(h + u) % NY, b, at, kk]

    wxsem, wrsem, wssem = group(), group(), group()

    def wx(u):
        for b in range(2):
            send(wblock(u, b, x), wblock(u, b, x), w3sem.at[2 * b, u], cidx(z, xr, kk), h, wxsem)
            send(wblock(u, 1 - b, x), wblock(u, 1 - b, x), w3sem.at[1 + b, u], cidx(z, xl, kk), h, wxsem)

    def wrelay(u):
        arrived(wblock(u, 0, xl), w3sem.at[0, u])
        send(wblock(u, 0, xl), wblock(u, 0, xl), w3sem.at[3, u], cidx(z, xr, kk), h, wrsem)
        arrived(wblock(u, 1, xr), w3sem.at[1, u])
        send(wblock(u, 1, xr), wblock(u, 1, xr), w3sem.at[3, u], cidx(z, xl, kk), h, wrsem)

    def wsib(u, n):
        ref = wbuf.at[(h + u) % NY, :, (x, xl, xr, xo)[n], kk]
        send(ref, ref, w4sem.at[u], sib, h, wssem)

    def wneighbours(u):
        arrived(wbuf.at[(h + u) % NY, :, xl, kk], w3sem.at[2, u])
        wsib(u, 1)
        wsib(u, 2)

    def wopposite(u):
        arrived(wbuf.at[(h + u) % NY, :, xo, kk], w3sem.at[3, u])
        wsib(u, 3)

    def input_part(u):
        o = (h + u) % NY
        arrived(wbuf.at[o, :, :, 1 - kk], w4sem.at[u])

        def step(i, carry):
            b, x0 = i // 2, 2 * (i % 2)
            w = wbuf[o, b, pl.ds(x0, 2)].reshape(256, 512)
            p = mm(pair(vgall, o, 0, 2), w[:, :256], NT) + mm(pair(vgall, o, 2, 2), w[:, 256:], NT)
            if u == 3:
                ist[i] = (acc[i] + p).astype(BF16)
            else:
                acc[i] = p if u == 0 else acc[i] + p
            return carry
        lax.fori_loop(0, 4, step, 0)

    partial(0)
    zfirst(0)
    arrived(wz.at[pl.ds(0, 6)], w2sem)
    for u in range(NY):
        wx(u)
    for u in range(NY):
        wsib(u, 0)
    transposed_part(vh, gh, qh, kloc)
    lax.fori_loop(0, 4, key_step, 0)
    put(ks, k_out, 0)

    for j in range(2):
        arrived(vgall.at[yl, j], ysem.at[0, j])
        send(vgall.at[yl, j], vgall.at[yl, j], ysem.at[2, j], c, yr, yrsem)
        arrived(vgall.at[yr, 2 + j], ysem.at[1, 2 + j])
        send(vgall.at[yr, 2 + j], vgall.at[yr, 2 + j], ysem.at[2, 2 + j], c, yl, yrsem)
    forward(1)
    partial(1)
    zfirst(1)
    straight_part(gh, vh, kh, qloc)
    scan_done(o3k, 1)
    lax.fori_loop(0, 4, query_step, 0)
    put(qs, q_out, 0)
    wrelay(0)
    wrelay(1)

    for j in range(2):
        arrived(vgall.at[yl, 2 + j], ysem.at[0, 2 + j])
        arrived(vgall.at[yr, j], ysem.at[1, j])
    forward(2)
    partial(2)
    xsend1(2)
    wrelay(2)
    wrelay(3)
    xnext(0)
    wneighbours(0)
    wneighbours(1)

    for j in (0, 2):
        arrived(vgall.at[yo, j], ysem.at[2, j])
    forward(3)
    partial(3)
    xsend1(3)
    xsend2(2)
    for j in (1, 3):
        arrived(vgall.at[yo, j], ysem.at[2, j])
    forward(4)
    partial(4)
    xsend1(4)
    xlast(0)
    wneighbours(2)
    wneighbours(3)
    xdone(2)
    xsend2(3)
    xsend2(4)
    xnext(1)
    wopposite(0)
    wopposite(1)
    input_part(0)
    xdone(3)
    xdone(4)
    wopposite(2)
    wopposite(3)
    xlast(1)
    input_part(1)
    zdone(2)
    input_part(2)
    zdone(3)
    zdone(4)
    input_part(3)
    for i in range(4):
        put(ist.at[i], i_out.at[:, pl.ds(256 * i, 256)], 1)
    sent(vgall.at[pl.ds(0, 2)], wxsem)
    sent(vgall.at[0], wrsem)
    sent(vgall, wssem)
    sent(vsib.at[pl.ds(0, 3)], xgsem)
    sent(zs.at[pl.ds(0, 2), pl.ds(0, 7)], zgsem)
    sent(fr.at[pl.ds(0, 3)], fgsem)

    @pl.when(mine)
    def _():
        arrived(fr.at[pl.ds(0, 3)], fsem)

    @pl.when(jnp.logical_not(mine))
    def _():
        arrived(fr, fsem)

    for n in range(4):
        put(fr.at[n], w_out.at[pl.ds(32 * (n % 2), 32), pl.ds(256 * (n // 2), 256)], 2)
    arrived(vgall.at[pl.ds(0, 2)], osem.at[0])
    arrived(ist, osem.at[1])
    arrived(fr, osem.at[2])
    for cond, desc in pending:
        if cond is None:
            desc.wait()
        else:
            pl.when(cond)(desc.wait_send)


def write_out(q_in, k_in, i_in, w_in, q_out, k_out, i_out, w_out, sems):
    pairs = ((i_in, i_out), (q_in, q_out), (k_in, k_out), (w_in, w_out))
    copies = [pltpu.make_async_copy(src, dst, sems.at[n]) for n, (src, dst) in enumerate(pairs)]
    for copy in copies:
        copy.start()
    for copy in copies:
        copy.wait()


def local(queries, keys, values, out_grad, inputs, value_weight):
    length = queries.shape[0]
    tokens = length * lax.axis_size("ctx")
    factor = 1.0 / math.sqrt(DH * tokens)
    wscale = 1.0 / math.sqrt(tokens)
    vm = pltpu.VMEM
    dma = pltpu.SemaphoreType.DMA
    scratch = [
        vm((4, 512, 128), BF16), vm((4, 512, 128), BF16), vm((4, 512, 128), BF16), vm((4, 512, 128), BF16),
        vm((2, 512, 1024), BF16), vm((2, 1024, 512), BF16),
        vm((8, 64, 512), BF16), vm((4, 2, 4, 2, 64, 512), BF16),
        vm((4, 128, 128), F32), vm((4, 128, 128), F32),
        vm((8, 64, 128), F32), vm((8, 64, 128), F32),
        vm((8, 64, 128), F32), vm((8, 64, 128), F32),
        vm((64, 128), BF16), vm((64, 128), BF16),
        vm((8, 64, 128), BF16), vm((8, 64, 128), BF16),
        vm((64, 128), F32), vm((64, 128), F32),
        vm((8, 64, 128), BF16), vm((8, 64, 128), BF16),
        vm((4, 128, 128), BF16), vm((4, 128, 128), BF16),
        vm((4, 512, 128), F32), vm((4, 512, 128), F32), vm((4, 512, 128), F32),
        vm((4, 4, 512, 128), BF16), vm((5, 2, 512, 128), BF16),
        vm((5, 4, 2, 128, 256), F32), vm((4, 512, 256), F32),
        vm((5, 2, 128, 256), BF16), vm((5, 2, 128, 256), BF16), vm((5, 2, 128, 256), BF16),
        vm((5, 2, 128, 256), BF16), vm((5, 2, 128, 256), BF16), vm((5, 2, 128, 256), BF16),
        vm((5, 8, 32, 256), BF16), vm((5, 8, 32, 256), BF16),
        vm((2, 8, 4, 32, 256), BF16), vm((2, 8, 4, 32, 256), BF16), vm((2, 4, 32, 256), BF16), vm((2, 4, 32, 256), BF16),
        vm((5, 32, 256), F32), vm((4, 32, 256), F32),
        vm((512, 512), BF16), vm((512, 512), BF16), vm((4, 512, 256), BF16),
        dma((6,)), dma((40,)), dma((2,)), dma((2, 8)), dma((2,)),
        dma((2, 5)), dma(()), dma((4, 4)), dma((4,)), dma(()), dma((3, 4)), dma((5,)), dma((3, 5)),
        dma((5,)), dma(()), dma((3,)),
    ]
    out_shape = (
        pltpu.VMEM((512, 512), BF16),
        pltpu.VMEM((512, 512), BF16),
        pltpu.VMEM((512, 1024), BF16),
        pltpu.VMEM((64, 512), F32),
    )
    results = pl.pallas_call(
        functools.partial(kernel, factor, wscale),
        out_shape=out_shape,
        in_specs=[pl.BlockSpec(memory_space=pl.ANY)] * 6,
        out_specs=[pl.BlockSpec(memory_space=pl.ANY)] * 4,
        scratch_shapes=scratch,
        compiler_params=pltpu.CompilerParams(
            collective_id=0, has_side_effects=True, vmem_limit_bytes=56 * 1024 * 1024),
        name="attention_backward",
    )(queries, keys, values, out_grad, inputs, value_weight)
    return pl.pallas_call(
        write_out,
        out_shape=tuple(jax.ShapeDtypeStruct(r.shape, r.dtype) for r in results),
        in_specs=[pl.BlockSpec(memory_space=pltpu.VMEM)] * 4,
        out_specs=[pl.BlockSpec(memory_space=pl.ANY)] * 4,
        scratch_shapes=[dma((4,))],
        name="write_out",
    )(*(pltpu.with_memory_space_constraint(r, pltpu.VMEM) for r in results))


def solution(mesh):
    spec = P("ctx", "head")
    return jax.shard_map(
        local, mesh=mesh, in_specs=(spec,) * 6, out_specs=(spec,) * 4, check_vma=False)
```

time: 112 us -> 74.9 us (0.67)
  Pallas kernels: 105 us -> 73.3 us
  local copies, waits for them, and re-layouts: 5.5 us -> 0 us
    pallas_call x1, Pallas kernels: 105 us -> 71.9 us  [local(): pl.pallas_call(functools.partial(kernel, factor, wscale), out_shape=out_s...]
    unnamed x8 -> x0, local copies, waits for them, and re-layouts: 5.5 us -> none
    pallas_call x0 -> x1, Pallas kernels: none -> 1.38 us  [local(): pl.pallas_call(write_out, out_shape=tuple((jax.ShapeDtypeStruct(r.shape,...]
where the time goes in v2:
time: 74.9 us; the launch traced here: 73.9 us
  Pallas kernels  73.3 us (98%)
    pallas_call x1, Pallas kernels, local(): pl.pallas_call(functools.partial(kernel, factor, wscale), out_shape=out_s...  71.9 us

profile of v2, /device:TPU:17, one launch (start us, length us, event | category | flops | bytes accessed | tf_op | source)
XLA Modules:
  0.0 73.9 jit_solution(7527807304973522524)
XLA Ops:
  0.6 71.9 %attention_backward.1 = (bf16[512,512]{1,0:T(8,128)(2,1)S(1)}, bf16[512,512]{1,0:T(8,128)(2,1)S(1)}, bf16[512,1024]{1,0:T(8,128)(2,1)S(1)}, f32[64,512]{1,0:T(8,128)S(1)}) custom-call(bf16[512,512]{1,0:T(8,128)(2,1)} %q_hbm.1, bf16[512,512]{1,0:T(8,128)(2,1)} %k_hbm.1, bf16[512,512]{1,0:T(8,128)(2,1)} %v_hbm.1, bf16[512,512]{1,0:T(8,128)(2,1)} %g_hbm.1, ...), custom_call_target="tpu_custom_call" | custom-call | tf_op jit(solution)/shard_map/attention_backward/pallas_call | solution.py:599
  72.6 1.4 %write_out.1 = (bf16[512,512]{1,0:T(8,128)(2,1)}, bf16[512,512]{1,0:T(8,128)(2,1)}, bf16[512,1024]{1,0:T(8,128)(2,1)}, f32[64,512]{1,0:T(8,128)}) custom-call(bf16[512,512]{1,0:T(8,128)(2,1)S(1)} %get-tuple-element.8.q_in, bf16[512,512]{1,0:T(8,128)(2,1)S(1)} %get-tuple-element.9.k_in, bf16[512,1024]{1,0:T(8,128)(2,1)S(1)} %get-tuple-element.10.i_in, ...), custom_call_target="tpu_custom_call" | custom-call | tf_op jit(solution)/shard_map/write_out/pallas_call | solution.py:609

commit v3 on v2

--- a/solution.py
+++ b/solution.py
@@ -104,10 +104,12 @@
         sk[j] = mm(kh[j].T, vh[j])
     pl.semaphore_wait(barrier, partners)
 
+    plane = [2 * ((x + dx) % NX) + (kk + dk) % 2 for dx, dk in
+             ((2, 0), (2, 1), (1, 0), (3, 0), (1, 1), (3, 1), (0, 1))]
+
     def scan1(s, r1, row):
         sem = group()
-        for off in range(1, 8):
-            to = (m + off) % 8
+        for to in plane:
             send(s.at[to // 2, pl.ds(pl.multiple_of(64 * (to % 2), 64), 64)], r1.at[m],
                  p1sem.at[row], z * 8 + to, h, sem)
         sent(r1.at[pl.ds(0, 7)], sem)
@@ -121,7 +123,7 @@
             ws[i] = total
             total = total + r1[i]
         t2[...] = total.astype(BF16)
-        for d in range(1, NZ):
+        for d in (4, 3, 5, 2, 6, 1, 7):
             zz = z - d if reverse else z + d
             cond = zz >= 0 if reverse else zz < NZ
             desc = send(t2, z2.at[d], p2sem.at[row, d], cidx(jnp.clip(zz, 0, NZ - 1), x, kk), h, group(), cond)
@@ -139,8 +141,7 @@
         for i in range(8):
             o3[i] = (ws[i] + za[...]).astype(BF16)
         sem = group()
-        for off in range(1, 8):
-            to = (m + off) % 8
+        for to in plane:
             send(o3.at[to], full.at[x, pl.ds(pl.multiple_of(64 * kk, 64), 64)],
                  p3sem.at[row], z * 8 + to, h, sem)
         sent(o3.at[pl.ds(0, 7)], sem)
@@ -166,7 +167,7 @@
 
     def wring1():
         load_w.wait()
-        for d in (1, 2):
+        for d in (2, 1):
             wz_to(z, w1sem.at[0, d], d)
             wz_to(z, w1sem.at[1, d], -d)
         wnext(z)
@@ -180,6 +181,8 @@
         wz_to(right, w1sem.at[0, 4], 2)
         wnext(right)
         wnext(left)
+
+    def wring2b():
         for side, at in ((0, (z + 7) % NZ), (1, (z + 1) % NZ)):
             arrived(wz.at[at], w1sem.at[side, 1])
             wnext(at)
@@ -235,13 +238,13 @@
     scan2(r1q, wsq, t2q, z2q, 0, True)
     wring2()
     transposed_part(kh, qh, gh, vloc)
+    wring2b()
     scan2(r1k, wsk, t2k, z2k, 1, False)
     transpose_inputs(0)
     arrived(inb.at[1], isem)
     transpose_inputs(1)
     scan3(wsq, z2q, zaq, o3q, later, 0, True)
     wring3()
-    scan3(wsk, z2k, zak, o3k, prior, 1, False)
 
     scan_done(o3q, 0)
     for j in range(4):
@@ -262,6 +265,7 @@
 
     origins = (h, pick(yl, yr), pick(yr, yl), yo, yo)
     sib_origins = (h, origins[2], origins[1], yo, yo)
+    senders = (h, pick(yr, yl), pick(yl, yr), yo, yo)
     heads = ((0, 1), (0, 1), (0, 1), (0,), (1,))
     cols = tuple(128 * len(js) for js in heads)
 
@@ -301,7 +305,7 @@
     def ways(e):
         return (xr, xl) if e == 2 else (xl, xr)
 
-    xgsem, zgsem, fgsem, zfsem, xfsem = group(), group(), group(), group(2), group(2)
+    xgsem, zgsem, zfsem, xfsem = group(), group(), group(2), group(2)
 
     def cut(ref, e):
         return ref.at[e, :, :, pl.ds(0, cols[e])]
@@ -330,32 +334,31 @@
             total = (part[e, x, b, r0:r0 + 32, :w] + rxb[e, b, r0:r0 + 32, :w].astype(F32)
                      + rxc[e, b, r0:r0 + 32, :w].astype(F32))
             zs[e, p, :, :w] = total.astype(BF16)
-        for dz in range(1, NZ):
+        for dz in (4, 3, 5, 2, 6, 1, 7, 0):
             to = (z + dz) % NZ
-            send(zs.at[e, to, :, pl.ds(0, w)], zr.at[e, z, :, pl.ds(0, w)], zsem.at[e], cidx(to, x, kk), h, zgsem)
-        zr[e, z, :, :w] = zs[e, z, :, :w]
-
-    mine = (h == z // 2) & (kk == z // 2 % 2)
+            send(zs.at[e, to, :, pl.ds(0, w)], zr.at[e, z, :, pl.ds(0, w)], zsem.at[e],
+                 cidx(to, x, kk), origins[e], zgsem)
+
+    mine = kk == z // 2 % 2
     slot = 2 * kk + z // 4
 
     def finish(e, total):
         w = cols[e]
         lo = 128 if e == 4 else 0
         fs[e, :, :w] = total * wscale
-        to = cidx(2 * h + z % 2, x, z // 2 % 2)
-        if e == 0:
-            other = jnp.logical_not(mine)
-            pending.append((other, send(fs.at[0], fr.at[slot], fsem, to, h, group(), other)))
-
-            @pl.when(mine)
-            def _():
-                fr[slot] = fs[0]
-        else:
-            send(fs.at[e, :, pl.ds(0, w)], fr.at[slot, :, pl.ds(lo, w)], fsem, to, origins[e], fgsem)
+        to = cidx(2 * senders[e] + z % 2, x, z // 2 % 2)
+        local = mine & (senders[e] == z // 2)
+        remote = jnp.logical_not(local)
+        pending.append((remote, send(fs.at[e, :, pl.ds(0, w)], fr.at[slot, :, pl.ds(lo, w)], fsem, to, h,
+                                     group(), remote)))
+
+        @pl.when(local)
+        def _():
+            fr[slot, :, lo:lo + w] = fs[e, :, :w]
 
     def zdone(e):
         w = cols[e]
-        arrived(zr.at[e, pl.ds(0, 7), :, pl.ds(0, w)], zsem.at[e])
+        arrived(zr.at[e, :, :, pl.ds(0, w)], zsem.at[e])
         total = zr[e, 0, :, :w].astype(F32)
         for zz in range(1, NZ):
             total = total + zr[e, zz, :, :w].astype(F32)
@@ -378,14 +381,17 @@
             for zz in range(1, NZ):
                 total = total + zfr[e, zz, xx].astype(F32)
             xfs[e, xx] = total.astype(BF16)
-        for dx in range(1, NX):
+        for dx in (2, 1, 3) if e == 0 else (2, 1, 3, 0):
             to = (x + dx) % NX
-            send(xfs.at[e, to], xfr.at[e, x], xsem.at[0, e], cidx(z, to, kk), h, xfsem[e])
-        xfr[e, x] = xfs[e, x]
-        sent(xfr.at[e, pl.ds(0, 3)], xfsem[e])
+            send(xfs.at[e, to], xfr.at[e, x], xsem.at[0, e], cidx(z, to, kk), origins[e], xfsem[e])
+        if e == 0:
+            xfr[e, x] = xfs[e, x]
+            sent(xfr.at[e, pl.ds(0, 3)], xfsem[e])
+        else:
+            sent(xfr.at[e], xfsem[e])
 
     def xlast(e):
-        arrived(xfr.at[e, pl.ds(0, 3)], xsem.at[0, e])
+        arrived(xfr.at[e, pl.ds(0, 3)] if e == 0 else xfr.at[e], xsem.at[0, e])
         total = xfr[e, 0].astype(F32)
         for xx in range(1, NX):
             total = total + xfr[e, xx].astype(F32)
@@ -455,6 +461,7 @@
     arrived(wz.at[pl.ds(0, 6)], w2sem)
     for u in range(NY):
         wx(u)
+    scan3(wsk, z2k, zak, o3k, prior, 1, False)
     for u in range(NY):
         wsib(u, 0)
     transposed_part(vh, gh, qh, kloc)
@@ -469,12 +476,9 @@
     forward(1)
     partial(1)
     zfirst(1)
-    straight_part(gh, vh, kh, qloc)
-    scan_done(o3k, 1)
-    lax.fori_loop(0, 4, query_step, 0)
-    put(qs, q_out, 0)
     wrelay(0)
     wrelay(1)
+    straight_part(gh, vh, kh, qloc)
 
     for j in range(2):
         arrived(vgall.at[yl, 2 + j], ysem.at[0, 2 + j])
@@ -482,43 +486,46 @@
     forward(2)
     partial(2)
     xsend1(2)
-    wrelay(2)
-    wrelay(3)
-    xnext(0)
-    wneighbours(0)
-    wneighbours(1)
 
     for j in (0, 2):
         arrived(vgall.at[yo, j], ysem.at[2, j])
     forward(3)
     partial(3)
     xsend1(3)
-    xsend2(2)
     for j in (1, 3):
         arrived(vgall.at[yo, j], ysem.at[2, j])
     forward(4)
     partial(4)
     xsend1(4)
+    xsend2(2)
+    xnext(0)
+    xsend2(3)
+    scan_done(o3k, 1)
+    lax.fori_loop(0, 4, query_step, 0)
+    put(qs, q_out, 0)
+    xsend2(4)
+    xnext(1)
+    wrelay(2)
+    wrelay(3)
+    wneighbours(0)
+    wneighbours(1)
+    wopposite(0)
+    wopposite(1)
+    xdone(2)
+    xdone(3)
+    input_part(0)
+    xdone(4)
     xlast(0)
+    input_part(1)
+    xlast(1)
+    zdone(2)
     wneighbours(2)
     wneighbours(3)
-    xdone(2)
-    xsend2(3)
-    xsend2(4)
-    xnext(1)
-    wopposite(0)
-    wopposite(1)
-    input_part(0)
-    xdone(3)
-    xdone(4)
     wopposite(2)
     wopposite(3)
-    xlast(1)
-    input_part(1)
-    zdone(2)
-    input_part(2)
     zdone(3)
     zdone(4)
+    input_part(2)
     input_part(3)
     for i in range(4):
         put(ist.at[i], i_out.at[:, pl.ds(256 * i, 256)], 1)
@@ -526,8 +533,7 @@
     sent(vgall.at[0], wrsem)
     sent(vgall, wssem)
     sent(vsib.at[pl.ds(0, 3)], xgsem)
-    sent(zs.at[pl.ds(0, 2), pl.ds(0, 7)], zgsem)
-    sent(fr.at[pl.ds(0, 3)], fgsem)
+    sent(zs.at[pl.ds(0, 2)], zgsem)
 
     @pl.when(mine)
     def _():

time: 74.9 us -> 71.2 us (0.951); the launches traced: 73.9 us -> 71.1 us
  Pallas kernels: 73.3 us -> 70.4 us
    pallas_call x1, Pallas kernels: 71.9 us -> 69 us  [local(): pl.pallas_call(functools.partial(kernel, factor, wscale), out_shape=out_s...]
where the time goes in v3:
time: 71.2 us; the launch traced here: 71.1 us
  Pallas kernels  70.4 us (99%)
    pallas_call x1, Pallas kernels, local(): pl.pallas_call(functools.partial(kernel, factor, wscale), out_shape=out_s...  69 us

profile of v3, /device:TPU:17, one launch (start us, length us, event | category | flops | bytes accessed | tf_op | source)
XLA Modules:
  0.0 71.1 jit_solution(15818903039697886624)
XLA Ops:
  0.6 69.0 %attention_backward.1 = (bf16[512,512]{1,0:T(8,128)(2,1)S(1)}, bf16[512,512]{1,0:T(8,128)(2,1)S(1)}, bf16[512,1024]{1,0:T(8,128)(2,1)S(1)}, f32[64,512]{1,0:T(8,128)S(1)}) custom-call(bf16[512,512]{1,0:T(8,128)(2,1)} %q_hbm.1, bf16[512,512]{1,0:T(8,128)(2,1)} %k_hbm.1, bf16[512,512]{1,0:T(8,128)(2,1)} %v_hbm.1, bf16[512,512]{1,0:T(8,128)(2,1)} %g_hbm.1, ...), custom_call_target="tpu_custom_call" | custom-call | tf_op jit(solution)/shard_map/attention_backward/pallas_call | solution.py:605
  69.7 1.4 %write_out.1 = (bf16[512,512]{1,0:T(8,128)(2,1)}, bf16[512,512]{1,0:T(8,128)(2,1)}, bf16[512,1024]{1,0:T(8,128)(2,1)}, f32[64,512]{1,0:T(8,128)}) custom-call(bf16[512,512]{1,0:T(8,128)(2,1)S(1)} %get-tuple-element.8.q_in, bf16[512,512]{1,0:T(8,128)(2,1)S(1)} %get-tuple-element.9.k_in, bf16[512,1024]{1,0:T(8,128)(2,1)S(1)} %get-tuple-element.10.i_in, ...), custom_call_target="tpu_custom_call" | custom-call | tf_op jit(solution)/shard_map/write_out/pallas_call | solution.py:615

commit v4 on v3

--- a/solution.py
+++ b/solution.py
@@ -503,29 +503,28 @@
     scan_done(o3k, 1)
     lax.fori_loop(0, 4, query_step, 0)
     put(qs, q_out, 0)
+    for u in range(2):
+        wneighbours(u)
+        wopposite(u)
     xsend2(4)
+    input_part(0)
+    xdone(2)
+    xdone(3)
+    xlast(0)
     xnext(1)
     wrelay(2)
     wrelay(3)
-    wneighbours(0)
-    wneighbours(1)
-    wopposite(0)
-    wopposite(1)
-    xdone(2)
-    xdone(3)
-    input_part(0)
     xdone(4)
-    xlast(0)
     input_part(1)
-    xlast(1)
-    zdone(2)
     wneighbours(2)
     wneighbours(3)
+    xlast(1)
     wopposite(2)
     wopposite(3)
+    zdone(2)
+    input_part(2)
     zdone(3)
     zdone(4)
-    input_part(2)
     input_part(3)
     for i in range(4):
         put(ist.at[i], i_out.at[:, pl.ds(256 * i, 256)], 1)

time: 71.2 us -> 71 us (level)
  no operation moved by 1% of the time
where the time goes in v4:
time: 71 us; the launch traced here: 70.9 us
  Pallas kernels  70.2 us (99%)
    pallas_call x1, Pallas kernels, local(): pl.pallas_call(functools.partial(kernel, factor, wscale), out_shape=out_s...  68.8 us

profile of v4, /device:TPU:17, one launch (start us, length us, event | category | flops | bytes accessed | tf_op | source)
XLA Modules:
  0.0 70.9 jit_solution(7062789705547249371)
XLA Ops:
  0.6 68.8 %attention_backward.1 = (bf16[512,512]{1,0:T(8,128)(2,1)S(1)}, bf16[512,512]{1,0:T(8,128)(2,1)S(1)}, bf16[512,1024]{1,0:T(8,128)(2,1)S(1)}, f32[64,512]{1,0:T(8,128)S(1)}) custom-call(bf16[512,512]{1,0:T(8,128)(2,1)} %q_hbm.1, bf16[512,512]{1,0:T(8,128)(2,1)} %k_hbm.1, bf16[512,512]{1,0:T(8,128)(2,1)} %v_hbm.1, bf16[512,512]{1,0:T(8,128)(2,1)} %g_hbm.1, ...), custom_call_target="tpu_custom_call" | custom-call | tf_op jit(solution)/shard_map/attention_backward/pallas_call | solution.py:604
  69.5 1.4 %write_out.1 = (bf16[512,512]{1,0:T(8,128)(2,1)}, bf16[512,512]{1,0:T(8,128)(2,1)}, bf16[512,1024]{1,0:T(8,128)(2,1)}, f32[64,512]{1,0:T(8,128)}) custom-call(bf16[512,512]{1,0:T(8,128)(2,1)S(1)} %get-tuple-element.8.q_in, bf16[512,512]{1,0:T(8,128)(2,1)S(1)} %get-tuple-element.9.k_in, bf16[512,1024]{1,0:T(8,128)(2,1)S(1)} %get-tuple-element.10.i_in, ...), custom_call_target="tpu_custom_call" | custom-call | tf_op jit(solution)/shard_map/write_out/pallas_call | solution.py:614

commit v5 on v4

--- a/solution.py
+++ b/solution.py
@@ -555,7 +555,9 @@
 
 
 def write_out(q_in, k_in, i_in, w_in, q_out, k_out, i_out, w_out, sems):
-    pairs = ((i_in, i_out), (q_in, q_out), (k_in, k_out), (w_in, w_out))
+    pairs = [(src.at[pl.ds(at, 128)], dst.at[pl.ds(at, 128)])
+             for at in range(0, 512, 128) for src, dst in ((i_in, i_out), (q_in, q_out), (k_in, k_out))]
+    pairs.append((w_in, w_out))
     copies = [pltpu.make_async_copy(src, dst, sems.at[n]) for n, (src, dst) in enumerate(pairs)]
     for copy in copies:
         copy.start()
@@ -616,7 +618,7 @@
         out_shape=tuple(jax.ShapeDtypeStruct(r.shape, r.dtype) for r in results),
         in_specs=[pl.BlockSpec(memory_space=pltpu.VMEM)] * 4,
         out_specs=[pl.BlockSpec(memory_space=pl.ANY)] * 4,
-        scratch_shapes=[dma((4,))],
+        scratch_shapes=[dma((13,))],
         name="write_out",
     )(*(pltpu.with_memory_space_constraint(r, pltpu.VMEM) for r in results))
 

time: 71 us -> 71 us (level)
  no operation moved by 1% of the time
where the time goes in v5:
time: 71 us; the launch traced here: 70.9 us
  Pallas kernels  70.3 us (99%)
    pallas_call x1, Pallas kernels, local(): pl.pallas_call(functools.partial(kernel, factor, wscale), out_shape=out_s...  68.8 us
    pallas_call x1, Pallas kernels, local(): pl.pallas_call(write_out, out_shape=tuple((jax.ShapeDtypeStruct(r.shape,...  1.46 us

profile of v5, /device:TPU:17, one launch (start us, length us, event | category | flops | bytes accessed | tf_op | source)
XLA Modules:
  0.0 70.9 jit_solution(12390801531993669689)
XLA Ops:
  0.6 68.8 %attention_backward.1 = (bf16[512,512]{1,0:T(8,128)(2,1)S(1)}, bf16[512,512]{1,0:T(8,128)(2,1)S(1)}, bf16[512,1024]{1,0:T(8,128)(2,1)S(1)}, f32[64,512]{1,0:T(8,128)S(1)}) custom-call(bf16[512,512]{1,0:T(8,128)(2,1)} %q_hbm.1, bf16[512,512]{1,0:T(8,128)(2,1)} %k_hbm.1, bf16[512,512]{1,0:T(8,128)(2,1)} %v_hbm.1, bf16[512,512]{1,0:T(8,128)(2,1)} %g_hbm.1, ...), custom_call_target="tpu_custom_call" | custom-call | tf_op jit(solution)/shard_map/attention_backward/pallas_call | solution.py:606
  69.5 1.5 %write_out.1 = (bf16[512,512]{1,0:T(8,128)(2,1)}, bf16[512,512]{1,0:T(8,128)(2,1)}, bf16[512,1024]{1,0:T(8,128)(2,1)}, f32[64,512]{1,0:T(8,128)}) custom-call(bf16[512,512]{1,0:T(8,128)(2,1)S(1)} %get-tuple-element.8.q_in, bf16[512,512]{1,0:T(8,128)(2,1)S(1)} %get-tuple-element.9.k_in, bf16[512,1024]{1,0:T(8,128)(2,1)S(1)} %get-tuple-element.10.i_in, ...), custom_call_target="tpu_custom_call" | custom-call | tf_op jit(solution)/shard_map/write_out/pallas_call | solution.py:616
